TPU v7x, 128 devices: a whole 4x4x4 slice. The times are simulated.
128 devices in a mesh: grp: 4 (over z), sub: 4 (over y), dev: 8 (over x, core).
Axes of the slice: x: 4, y: 4, z: 4, core: 2. Of those that a mesh axis runs over, the one named last changes fastest.
Arguments:
- queries: bfloat16 [4, 32, 512, 1024], P('grp', ('sub', 'dev')), may hold values from -8 to 8
- cached: bfloat16 [4, 32, 4096, 256], P('grp', ('sub', 'dev')), may hold values from -4.5 to 4.5
- new_entries: bfloat16 [4, 32, 512, 256], P('grp', ('sub', 'dev')), may hold values from -4.5 to 4.5
- lengths: int32 [32], P(('sub', 'dev')), may hold values from 1024 to 4096
- residual: bfloat16 [32, 512, 2048], P(('sub', 'dev'), 'grp'), may hold values from -6 to 6
- w_out: bfloat16 [4096, 2048], P('grp'), may hold values from -0.1875 to 0.1875
- norm_gain: float32 [2048], replicated, may hold values from 0.5 to 1.5
- w_gate_up: bfloat16 [128, 2048, 1536], P(('grp', 'sub', 'dev')), may hold values from -0.125 to 0.125
- w_down: bfloat16 [128, 768, 2048], P(('grp', 'sub', 'dev')), may hold values from -0.21875 to 0.21875
- routes: int32 [32, 512, 8], P(('sub', 'dev'), 'grp'), may hold values from 0 to 127, all different within a row; in each aligned block of 128 rows (0 to 127, 128 to 255, ..., all dimensions but the last counted through in order) at most 12 rows name the same one
- gate_codes: int32 [32, 512, 8], P(('sub', 'dev'), 'grp'), may hold values from 1 to 16
Outputs:
- attn_out: bfloat16 [32, 512, 2048], P(('sub', 'dev'), 'grp')
- mixed: bfloat16 [32, 512, 2048], P(('sub', 'dev'), 'grp')
Inputs may be any that keep to these rules, and one draw needn't show every extreme that they name: `routes`: each row names 8 different experts; within the rows of one device (aligned blocks of 128 rows in the order of requests, then rows) no expert is named by more than 12 rows.
All inputs are finite; a program needn't handle non-finite values.
Results may differ from a plain program's by a relative error of at most 0.0052.
Values may be sent and summed in bfloat16 or wider, within the bound.
A program may use at most 128 MiB of HBM per device.

v0:
```python
import jax
import jax.numpy as jnp
from jax import lax
from jax.sharding import PartitionSpec as P

TOP = 8


def in_blocks(shard, dim, peers):
    before, after = (shard.shape[:dim], shard.shape[dim + 1 :])
    return jnp.moveaxis(shard.reshape(*before, peers, -1, *after), dim, 0)


def sent_and_summed(shard, axis, dim):
    parts = in_blocks(shard, dim, lax.axis_size(axis))
    arrived = lax.all_to_all(parts, axis, split_axis=0, concat_axis=0, tiled=True)
    return arrived.sum(axis=0)


def attend(query_rows, cached_rows, entry_rows, length):
    head_width = cached_rows.shape[1] // 2
    stored = cached_rows.shape[0]
    span_len = entry_rows.shape[0]
    key_rows = jnp.concatenate([cached_rows[:, :head_width], entry_rows[:, :head_width]], axis=0)
    value_rows = jnp.concatenate([cached_rows[:, head_width:], entry_rows[:, head_width:]], axis=0)
    position = jnp.arange(stored + span_len, dtype=jnp.int32)[None, :]
    row_index = jnp.arange(span_len, dtype=jnp.int32)[:, None]
    visible = jnp.where(position < stored, position < length, position - stored <= row_index)
    head_queries = query_rows.reshape(span_len, -1, head_width).transpose(1, 0, 2)

    def one_head(head_rows):
        scores = jnp.dot(
            head_rows, key_rows.T, preferred_element_type=jnp.float32
        ) * head_width ** (-0.5)
        scores = jnp.where(visible, scores, -1e30)
        row_peak = jnp.max(scores, axis=1, keepdims=True)
        exponent = jnp.exp(scores - row_peak)
        totals = jnp.sum(exponent, axis=1, keepdims=True)
        weighted = jnp.dot(
            exponent.astype(jnp.bfloat16), value_rows, preferred_element_type=jnp.float32
        )
        return (weighted / totals).astype(jnp.bfloat16)

    outputs = lax.map(one_head, head_queries)
    return outputs.transpose(1, 0, 2).reshape(span_len, -1)


def per_device(
    queries,
    cached,
    new_entries,
    lengths,
    residual,
    w_out,
    norm_gain,
    w_gate_up,
    w_down,
    routes,
    gate_codes,
):
    width = residual.shape[2]
    own_rows = residual.shape[1]
    attended = attend(queries[0, 0], cached[0, 0], new_entries[0, 0], lengths[0])
    total = jnp.dot(attended, w_out, preferred_element_type=jnp.float32)
    attn_sum = sent_and_summed(total, "grp", 0)
    attn_out = attn_sum.astype(jnp.bfloat16)
    state = residual[0].astype(jnp.float32) + attn_sum
    scale_inv = lax.rsqrt(jnp.mean(state * state, axis=1, keepdims=True) + 1e-06)
    normed = (state * scale_inv * norm_gain[None, :]).astype(jnp.bfloat16)
    groups = lax.axis_size("grp")
    subgroups = lax.axis_size("sub")
    members = lax.axis_size("dev")
    devices = groups * subgroups * members
    local_experts = w_gate_up.shape[0]
    expert_total = local_experts * devices
    hidden_width = w_down.shape[1]
    capacity = max(2, own_rows * TOP * 3 // (2 * expert_total))
    codes_float = gate_codes[0].astype(jnp.float32)
    route_weight = codes_float / jnp.sum(codes_float, axis=-1, keepdims=True)
    flat_routes = routes[0].reshape(-1)
    assigned = flat_routes.shape[0]
    one_hot = (flat_routes[:, None] == jnp.arange(expert_total, dtype=jnp.int32)[None, :]).astype(
        jnp.int32
    )
    earlier_hits = jnp.cumsum(one_hot, axis=0) - one_hot
    rank_within = jnp.sum(earlier_hits * one_hot, axis=1)
    slot_index = flat_routes * capacity + rank_within
    slot_token = (
        jnp.zeros((expert_total * capacity,), jnp.int32)
        .at[slot_index]
        .set(jnp.arange(assigned, dtype=jnp.int32) // TOP)
    )
    filled = jnp.zeros((expert_total * capacity,), jnp.bool_).at[slot_index].set(True)
    outgoing = jnp.where(filled[:, None], normed[slot_token], jnp.zeros((), jnp.bfloat16))
    received = lax.all_to_all(
        outgoing.reshape(devices, -1, width),
        ("grp", "sub", "dev"),
        split_axis=0,
        concat_axis=0,
        tiled=True,
    )
    batches = received.reshape(devices, local_experts, capacity, width)
    projected = jnp.einsum("secd,edf->secf", batches, w_gate_up, preferred_element_type=jnp.float32)
    expert_hidden = (
        jax.nn.silu(projected[..., :hidden_width]) * projected[..., hidden_width:]
    ).astype(jnp.bfloat16)
    expert_out = jnp.einsum(
        "secf,efd->secd", expert_hidden, w_down, preferred_element_type=jnp.float32
    )
    produced = expert_out.astype(jnp.bfloat16).reshape(devices, -1, width)
    returned = lax.all_to_all(
        produced, ("grp", "sub", "dev"), split_axis=0, concat_axis=0, tiled=True
    )
    returned_flat = returned.reshape(-1, width)
    picked = returned_flat[slot_index].reshape(own_rows, TOP, width).astype(jnp.float32)
    moe_total = jnp.sum(picked * route_weight[:, :, None], axis=1)
    mixed = (state + moe_total).astype(jnp.bfloat16)
    return (attn_out[None], mixed[None])


def solution(mesh):
    placed = (
        P("grp", ("sub", "dev"), None, None),
        P("grp", ("sub", "dev"), None, None),
        P("grp", ("sub", "dev"), None, None),
        P(("sub", "dev")),
        P(("sub", "dev"), "grp", None),
        P("grp", None),
        P(),
        P(("grp", "sub", "dev"), None, None),
        P(("grp", "sub", "dev"), None, None),
        P(("sub", "dev"), "grp", None),
        P(("sub", "dev"), "grp", None),
    )
    return jax.shard_map(
        per_device,
        mesh=mesh,
        in_specs=placed,
        out_specs=(P(("sub", "dev"), "grp", None), P(("sub", "dev"), "grp", None)),
        check_vma=False,
    )
```

profile of v0, /device:TPU:90, one launch (start us, length us, event | category | flops | bytes accessed | tf_op | source)
XLA Modules:
  0.0 464.1 jit_solution(6974393751814606998)
XLA Ops:
  0.7 2.5 copy.26
  3.1 1.0 fusion.56
  4.1 1.7 fusion.55
  6.5 1.6 pad_maximum_fusion
  8.0 62.2 %while.11 = (s32[]{:T(128)}, bf16[8,512,128]{2,1,0:T(8,128)(2,1)}, bf16[8,512,128]{1,2,0:T(8,128)(2,1)}, bf16[4608,128]{1,0:T(8,128)(2,1)}, bf16[4608,128]{1,0:T...) while((s32[]{:T(128)}, bf16[8,512,128]{2,1,0:T(8,128)(2,1)}, ...), condition=%wide.region_3.4_spmd.clone, body=%wide.region_0.3_spmd.clone.sunk | while | flops 1229323264 | bytes 35689608 | solution.py:44
  8.0 4.3 fusion.69
  12.3 1.4 fusion.70
  13.7 2.1 fusion.71
  15.8 4.3 fusion.69
  20.1 1.4 fusion.70
  21.5 2.1 fusion.71
  23.6 4.3 fusion.69
  27.8 1.4 fusion.70
  29.3 2.1 fusion.71
  31.3 4.3 fusion.69
  35.6 1.4 fusion.70
  37.0 2.1 fusion.71
  39.1 4.3 fusion.69
  43.4 1.4 fusion.70
  44.8 2.1 fusion.71
  46.9 4.3 fusion.69
  51.2 1.4 fusion.70
  52.6 2.1 fusion.71
  54.7 4.3 fusion.69
  58.9 1.4 fusion.70
  60.4 2.1 fusion.71
  62.4 4.3 fusion.69
  66.7 1.4 fusion.70
  68.1 2.1 fusion.71
  70.2 2.9 copy.28
  73.1 2.3 dot_general.21
  75.4 6.8 %fusion.33 = f32[4,128,2048]{2,1,0:T(8,128)} fusion(bf16[4,128,1024]{2,1,0:T(8,128)(2,1)} %dot_general.21, bf16[1024,2048]{1,0:T(8,128)(2,1)} %param.18), kind=kOutput, calls=%fused_computation.30 | convolution fusion | flops 2147483648 | bytes 9437184 | tf_op jit(solution)/shard_map/dot_general | solution.py:64
  82.2 5.1 %all-to-all-start = ((f32[4,128,2048]{2,1,0:T(8,128)}), f32[4,128,2048]{2,1,0:T(8,128)}, u32[]{:S(2)}, u32[]{:S(2)}) async-start(f32[4,128,2048]{2,1,0:T(8,128)} %fusion.33), calls=%async_computation | async-start | bytes 8388608 | tf_op jit(solution)/shard_map/all_to_all | solution.py:16
  87.3 0.1 copy.30
  87.4 0.1 eq.29
  87.6 0.1 copy.29
  87.7 0.1 mul.58
  87.8 0.1 copy.32
  87.9 0.2 fusion.43
  88.1 0.8 copy-done.4
  89.0 1.1 broadcast_add_fusion
  90.1 0.1 copy.33
  90.2 0.4 fusion.42
  90.6 4.8 %scatter_custom_fusion.1 = s32[1536]{0:T(1024)S(1)} fusion(s32[1024]{0:T(1024)S(1)} %bitcast.86, s32[1024]{0:T(1024)S(1)} %add_select_fusion, s32[]{:T(128)} %constant.34.clone.1), kind=kCustom, calls=%fused_computation.68 | custom fusion | bytes 6148 | tf_op jit(solution)/shard_map/scatter | solution.py:91
  95.4 4.3 scatter_custom_fusion
  99.7 0.1 broadcast_in_dim.70
  99.9 33.4 %all-to-all-done = f32[4,128,2048]{2,1,0:T(8,128)} async-done(((f32[4,128,2048]{2,1,0:T(8,128)}), f32[4,128,2048]{2,1,0:T(8,128)}, u32[]{:S(2)}, u32[]{:S(2)}) %all-to-all-start) | async-done | bytes 4194336 | tf_op jit(solution)/shard_map/all_to_all | solution.py:16
  133.3 3.6 reduce_sum.60
  136.9 1.6 multiply_reduce_fusion
  138.5 2.5 multiply_convert_fusion
  141.0 13.8 %gather_fusion = bf16[1536,2048]{1,0:T(8,128)(2,1)} fusion(bf16[128,2048]{1,0:T(8,128)(2,1)} %get-tuple-element.92, s32[2048]{0:T(1024)S(1)} %pad_clamp_fusion), kind=kCustom, calls=%fused_computation | custom fusion | bytes 12589056 | tf_op jit(solution)/shard_map/gather | solution.py:94
  154.8 10.6 %gather.9 = bf16[128,12,2048]{2,1,0:T(8,128)(2,1)} reshape(bf16[1536,2048]{1,0:T(8,128)(2,1)} %gather_fusion) | data formatting | bytes 12582912 | tf_op jit(solution)/shard_map/gather | solution.py:94
  165.4 7.3 %broadcast_select_fusion = bf16[128,12,2048]{2,1,0:T(8,128)(2,1)} fusion(bf16[128,12,2048]{2,1,0:T(8,128)(2,1)} %gather.9, pred[128,12]{1,0:T(8,128)(4,1)S(1)} %broadcast_in_dim.70), kind=kLoop, calls=%fused_computation.22 | loop fusion | flops 3145728 | bytes 12584448 | tf_op jit(solution)/shard_map/jit(_where)/select_n | solution.py:94
  172.6 103.5 %all_to_all.15 = bf16[128,12,2048]{2,1,0:T(8,128)(2,1)S(1)} all-to-all(bf16[128,12,2048]{2,1,0:T(8,128)(2,1)} %broadcast_select_fusion), channel_id=1, replica_groups=mesh['grp'=4,'sub'=4,'dev'=8] {'grp','sub','dev'}, dimensions={0} | all-to-all | bytes 12582912 | tf_op jit(solution)/shard_map/all_to_all | solution.py:95
  276.1 25.7 %fusion.27 = f32[128,1,12,1536]{3,0,2,1:T(8,128)} fusion(bf16[1,2048,1536]{2,1,0:T(8,128)(2,1)} %param.20, bf16[128,12,2048]{2,1,0:T(8,128)(2,1)S(1)} %all_to_all.15), kind=kOutput, calls=%fused_computation.26 | convolution fusion | flops 9663676416 | bytes 22020096 | tf_op jit(solution)/shard_map/secd,edf->secf/dot_general | solution.py:103
  301.9 9.5 %convolution_convert_fusion = bf16[128,12,2048]{2,0,1:T(8,128)(2,1)S(1)} fusion(bf16[1,768,2048]{2,1,0:T(8,128)(2,1)S(1)} %copy-done, f32[128,1,12,1536]{3,0,2,1:T(8,128)} %fusion.27), kind=kOutput, calls=%fused_computation.29 | convolution fusion | flops 4842061824 | bytes 18874368 | tf_op jit(solution)/shard_map/secf,efd->secd/dot_general | solution.py:107
  311.4 6.8 %copy.35 = bf16[128,12,2048]{2,1,0:T(8,128)(2,1)} copy(bf16[128,12,2048]{2,0,1:T(8,128)(2,1)S(1)} %convolution_convert_fusion) | data formatting | bytes 12582912 | tf_op jit(solution)/shard_map/convert_element_type | solution.py:110
  318.2 11.1 %all-to-all-start.2 = ((bf16[128,12,2048]{2,1,0:T(8,128)(2,1)}), bf16[128,12,2048]{2,1,0:T(8,128)(2,1)}, u32[]{:S(2)}, u32[]{:S(2)}) async-start(bf16[128,12,2048]{2,1,0:T(8,128)(2,1)} %copy.35), calls=%async_computation.2 | async-start | bytes 16777216 | tf_op jit(solution)/shard_map/all_to_all | solution.py:111
  329.3 0.1 copy.36
  329.4 103.6 %all-to-all-done.2 = bf16[128,12,2048]{2,1,0:T(8,128)(2,1)} async-done(((bf16[128,12,2048]{2,1,0:T(8,128)(2,1)}), bf16[128,12,2048]{2,1,0:T(8,128)(2,1)}, u32[]{:S(2)}, u32[]{:S(2)}) %all-to-all-start.2) | async-done | bytes 6291488 | tf_op jit(solution)/shard_map/all_to_all | solution.py:111
  433.1 10.7 %reshape.146 = bf16[1536,2048]{1,0:T(8,128)(2,1)} reshape(bf16[128,12,2048]{2,1,0:T(8,128)(2,1)} %all-to-all-done.2) | data formatting | bytes 12582912 | tf_op jit(solution)/shard_map/reshape | solution.py:114
  443.8 12.4 %gather_fusion.1 = bf16[1024,2048]{1,0:T(8,128)(2,1)} fusion(bf16[1536,2048]{1,0:T(8,128)(2,1)} %reshape.146, s32[1024]{0:T(1024)S(1)} %broadcast_clamp_fusion), kind=kCustom, calls=%fused_computation.1 | custom fusion | bytes 8392704 | tf_op jit(solution)/shard_map/gather | solution.py:115
  456.2 6.6 %fusion.23 = f32[128,2048]{1,0:T(8,128)S(1)} fusion(bf16[1024,2048]{1,0:T(8,128)(2,1)} %gather_fusion.1, f32[128,8]{1,0:T(8,128)S(1)} %copy.36), kind=kLoop, calls=%fused_computation.21 | loop fusion | flops 6029312 | bytes 5246976 | tf_op jit(solution)/shard_map/reduce_sum | solution.py:116
  462.9 1.0 fusion.39
  (46 shorter events, 0.3 us)
Async XLA Ops:
  0.6 301.2 %copy-start = (bf16[1,768,2048]{2,1,0:T(8,128)(2,1)S(1)}, bf16[1,768,2048]{2,1,0:T(8,128)(2,1)}, u32[]{:S(2)}) copy-start(bf16[1,768,2048]{2,1,0:T(8,128)(2,1)} %param.21) | copy-start | bytes 9437188
  12.3 1.4 copy-start.1
  20.1 1.4 copy-start.1
  27.8 1.4 copy-start.1
  35.6 1.4 copy-start.1
  43.4 1.4 copy-start.1
  51.1 1.4 copy-start.1
  58.9 1.4 copy-start.1
  66.7 1.4 copy-start.1
  82.2 5.1 %copy-start.5 = (s32[1,128,8]{1,2,0:T(8,128)S(1)}, s32[1,128,8]{1,2,0:T(8,128)}, u32[]{:S(2)}) copy-start(s32[1,128,8]{1,2,0:T(8,128)} %param.22) | copy-start | bytes 12292
  82.2 51.0 %all-to-all-start = ((f32[4,128,2048]{2,1,0:T(8,128)}), f32[4,128,2048]{2,1,0:T(8,128)}, u32[]{:S(2)}, u32[]{:S(2)}) async-start(f32[4,128,2048]{2,1,0:T(8,128)} %fusion.33), calls=%async_computation | async-start | bytes 8388608 | tf_op jit(solution)/shard_map/all_to_all | solution.py:16
  88.1 0.8 copy-start.4
  89.0 49.5 %copy-start.7 = (f32[2048]{0:T(1024)S(1)}, f32[2048]{0:T(1024)}, u32[]{:S(2)}) copy-start(f32[2048]{0:T(1024)} %param.19) | copy-start | bytes 24580
  318.2 11.1 %copy-start.6 = (s32[1,128,8]{1,2,0:T(8,128)S(1)}, s32[1,128,8]{1,2,0:T(8,128)}, u32[]{:S(2)}) copy-start(s32[1,128,8]{1,2,0:T(8,128)} %param.23) | copy-start | bytes 12292
  318.2 114.9 %all-to-all-start.2 = ((bf16[128,12,2048]{2,1,0:T(8,128)(2,1)}), bf16[128,12,2048]{2,1,0:T(8,128)(2,1)}, u32[]{:S(2)}, u32[]{:S(2)}) async-start(bf16[128,12,2048]{2,1,0:T(8,128)(2,1)} %copy.35), calls=%async_computation.2 | async-start | bytes 16777216 | tf_op jit(solution)/shard_map/all_to_all | solution.py:111
  456.2 6.6 %copy-start.2 = (f32[128,2048]{1,0:T(8,128)S(1)}, f32[128,2048]{1,0:T(8,128)}, u32[]{:S(2)}) copy-start(f32[128,2048]{1,0:T(8,128)} %reduce_sum.60) | copy-start | bytes 3145732
  456.2 6.7 %copy-start.3 = (bf16[1,128,2048]{2,1,0:T(8,128)(2,1)S(1)}, bf16[1,128,2048]{2,1,0:T(8,128)(2,1)}, u32[]{:S(2)}) copy-start(bf16[1,128,2048]{2,1,0:T(8,128)(2,1)} %param.17) | copy-start | bytes 1572868
where the time goes:
time: 473 us; the launch traced here: 464 us
  waiting for transfers between devices  137 us (29%)
  blocking collectives  103 us (22%)
  matrix products  92.9 us (20%)
  local copies, waits for them, and re-layouts  75.6 us (16%)
  other arithmetic  37.1 us (8%)
  starting transfers between devices  16.2 us (3%)
    all_to_all x1, waiting for transfers between devices, per_device(): lax.all_to_all(produced, ('grp', 'sub', 'dev'), split_axis=0, concat_axis...  104 us
    all_to_all x1, blocking collectives, per_device(): lax.all_to_all(outgoing.reshape(devices, -1, width), ('grp', 'sub', 'dev'...  103 us
    dot_general x8, matrix products, one_head(): jnp.dot(head_rows, key_rows.T, preferred_element_type=jnp.float32)  34.1 us
    all_to_all x1, waiting for transfers between devices, sent_and_summed(): lax.all_to_all(parts, axis, split_axis=0, concat_axis=0, tiled=True)  33.4 us
    dot_general x1, matrix products, per_device(): jnp.einsum('secd,edf->secf', batches, w_gate_up, preferred_element_type=j...  25.7 us
    gather x2, local copies, waits for them, and re-layouts, per_device(): normed[slot_token]  24.4 us
    dot_general x8, matrix products, one_head(): jnp.dot(exponent.astype(jnp.bfloat16), value_rows, preferred_element_type...  16.8 us
    gather x1, local copies, waits for them, and re-layouts, per_device(): returned_flat[slot_index].reshape(own_rows, TOP, width).astype(jnp.float32)  12.4 us
  transfers between devices with their start and end apart: 2, of which 2 were waited for; matrix products, arithmetic and copies ran while one was open for 3% of the time, Pallas kernels for 0%

commit v1 on v0

v1 whole, which is shorter than its diff:
```python
import functools

import jax
import jax.numpy as jnp
from jax import lax
from jax.experimental import pallas as pl
from jax.experimental.pallas import tpu as pltpu
from jax.sharding import PartitionSpec as P

MESH = pl.DeviceIdType.MESH
TOP = 8
D = 2048
FF = 768
HD = 128
HEADS = 8
CACHE = 4096
SPAN = 512
KEYS = CACHE + SPAN
BLOCK = 128
UNIT = 512
TILE = 512
SCALE = HD**-0.5 * 1.4426950408889634
HIDDEN = -1e30
DEVICES = 128
STRIDE = 91
MSG = 8
MSG_COLS = D + D // 2
CHUNK = 32
CHUNKS = DEVICES // CHUNK
BF = jnp.bfloat16
F32 = jnp.float32


def iota(shape, dim):
    return lax.broadcasted_iota(jnp.int32, shape, dim)


def rem(a, b):
    return lax.rem(a, jnp.int32(b))


def div(a, b):
    return lax.div(a, jnp.int32(b))


def peer(slot, sign):
    g, s, d = lax.axis_index("grp"), lax.axis_index("sub"), lax.axis_index("dev")
    o = rem(slot * STRIDE, DEVICES)
    og, os, ox, oc = rem(o, 4), rem(div(o, 4), 4), rem(div(o, 16), 4), div(o, 64)
    x = rem(div(d, 2) + sign * ox + 4, 4)
    c = rem(rem(d, 2) + oc, 2)
    return rem(g + sign * og + 4, 4), rem(s + sign * os + 4, 4), x * 2 + c


def dot(a, b):
    return jnp.dot(a, b, preferred_element_type=F32)


def attend_kernel(
    length, q_ref, cached, new, residual, gain, w_hbm,
    out_ref, state_ref, normed_ref,
    keys, values, queries, scores, probs, peaks, attended, w_ref, sent, arrived, own,
    w_sem, send_sem, recv_sem,
):
    g, s, d = lax.axis_index("grp"), lax.axis_index("sub"), lax.axis_index("dev")
    w_copy = pltpu.make_async_copy(w_hbm, w_ref, w_sem)
    w_copy.start()
    barrier = pltpu.get_barrier_semaphore()
    for step in range(1, 4):
        pl.semaphore_signal(barrier, inc=1, device_id=(rem(g + step, 4), s, d), device_id_type=MESH)

    ones = jnp.where(iota((TILE, HD), 1) == 0, 1.0, 0.0).astype(BF)

    @pl.loop(0, CACHE // TILE)
    def _(i):
        rows = pl.ds(pl.multiple_of(i * TILE, TILE), TILE)
        keys[0:HD, rows] = cached[rows, 0:HD].T
        unseen = (iota((HD, TILE), 0) == 0) & (i * TILE + iota((HD, TILE), 1) >= length[0])
        keys[HD:, rows] = jnp.where(unseen, HIDDEN, 0.0).astype(BF)
        values[rows, 0:HD] = cached[rows, HD:]
        values[rows, HD:] = ones

    keys[0:HD, CACHE:] = new[:, 0:HD].T
    keys[HD:, CACHE:] = jnp.zeros((HD, SPAN), BF)
    values[CACHE:, 0:HD] = new[:, HD:]
    values[CACHE:, HD:] = ones
    for slot in range(2):
        queries[slot, :, HD:] = jnp.where(iota((UNIT, HD), 1) == 0, 1.0, 0.0).astype(BF)

    def score(step, slot):
        block = rem(g + 1 + step, 4)
        rows = pl.ds(pl.multiple_of(block * BLOCK, BLOCK), BLOCK)
        for k in range(4):
            head = slot * 4 + k
            queries[slot, k * BLOCK : (k + 1) * BLOCK, 0:HD] = q_ref[rows, head * HD : (head + 1) * HD]
        q = queries[slot]
        peak = None
        for j in range(KEYS // TILE):
            tile = dot(q, keys[:, j * TILE : (j + 1) * TILE])
            if j * TILE >= CACHE:
                row = block * BLOCK + rem(iota((UNIT, TILE), 0), BLOCK)
                tile = jnp.where(iota((UNIT, TILE), 1) + (j * TILE - CACHE) <= row, tile, HIDDEN)
            scores[slot, :, j * TILE : (j + 1) * TILE] = tile
            for k in range(TILE // HD):
                part = tile[:, k * HD : (k + 1) * HD]
                peak = part if peak is None else jnp.maximum(peak, part)
        peaks[slot] = jnp.broadcast_to(jnp.max(peak, axis=1, keepdims=True), (UNIT, HD))

    def finish(slot):
        peak = peaks[slot]
        for k in range(KEYS // HD):
            cols = slice(k * HD, (k + 1) * HD)
            probs[:, cols] = jnp.exp2((scores[slot, :, cols] - peak) * SCALE).astype(BF)
        total = dot(probs[...], values[...])
        result = (total[:, 0:HD] / total[:, HD : HD + 1]).astype(BF)
        for k in range(4):
            head = slot * 4 + k
            attended[:, head * HD : (head + 1) * HD] = result[k * BLOCK : (k + 1) * BLOCK]

    def hand_over(step):
        block = rem(g + 1 + step, 4)
        return pltpu.make_async_remote_copy(
            src_ref=sent.at[step], dst_ref=arrived.at[step],
            send_sem=send_sem.at[step], recv_sem=recv_sem.at[step],
            device_id=(block, s, d), device_id_type=MESH,
        )

    score(0, 0)
    w_copy.wait()
    pl.semaphore_wait(barrier, 3)

    @pl.loop(0, 4)
    def _(step):
        score(step, 1)
        finish(0)
        score(jnp.minimum(step + 1, 3), 0)
        finish(1)
        own[...] = dot(attended[...], w_ref[...])

        @pl.when(step < 3)
        def _():
            sent[step] = own[...].astype(BF)
            hand_over(step).start()

    for step in range(3):
        hand_over(step).wait()
    attn_sum = own[...] + (arrived[0].astype(F32) + (arrived[1].astype(F32) + arrived[2].astype(F32)))
    out_ref[...] = attn_sum.astype(BF)
    state = residual[...].astype(F32) + attn_sum
    state_ref[...] = state
    inverse = lax.rsqrt(jnp.mean(state * state, axis=1, keepdims=True) + 1e-6)
    normed_ref[...] = (state * inverse * gain[...]).astype(BF)


def attend_and_norm(length, queries, cached, new, residual, gain, w_out):
    vmem = pl.BlockSpec(memory_space=pltpu.VMEM)
    block = (BLOCK, D)
    return pl.pallas_call(
        attend_kernel,
        out_shape=(
            jax.ShapeDtypeStruct(block, BF),
            jax.ShapeDtypeStruct(block, F32),
            jax.ShapeDtypeStruct(block, BF),
        ),
        in_specs=[pl.BlockSpec(memory_space=pltpu.SMEM)] + [vmem] * 5 + [pl.BlockSpec(memory_space=pl.ANY)],
        out_specs=(vmem, vmem, vmem),
        scratch_shapes=[
            pltpu.VMEM((2 * HD, KEYS), BF),
            pltpu.VMEM((KEYS, 2 * HD), BF),
            pltpu.VMEM((2, UNIT, 2 * HD), BF),
            pltpu.VMEM((2, UNIT, KEYS), F32),
            pltpu.VMEM((UNIT, KEYS), BF),
            pltpu.VMEM((2, UNIT, HD), F32),
            pltpu.VMEM((BLOCK, HEADS * HD), BF),
            pltpu.VMEM((HEADS * HD, D), BF),
            pltpu.VMEM((3, *block), BF),
            pltpu.VMEM((3, *block), BF),
            pltpu.VMEM(block, F32),
            pltpu.SemaphoreType.DMA,
            pltpu.SemaphoreType.DMA((3,)),
            pltpu.SemaphoreType.DMA((3,)),
        ],
        compiler_params=pltpu.CompilerParams(
            collective_id=0, has_side_effects=True, vmem_limit_bytes=56 << 20
        ),
        name="attend_and_norm",
    )(length, queries, cached, new, residual, gain, w_out)


def expert_kernel(
    normed, state, slot_of, weight_of, up_hbm, down_hbm,
    mixed, recv, ret,
    send, back, w_up, w_down, x_ref, part, total,
    w_sem, send_sem, recv_sem, back_sem, ret_sem, part_sem,
):
    up_copy = pltpu.make_async_copy(up_hbm, w_up, w_sem.at[0])
    down_copy = pltpu.make_async_copy(down_hbm, w_down, w_sem.at[1])
    up_copy.start()
    down_copy.start()
    barrier = pltpu.get_barrier_semaphore()

    @pl.loop(1, DEVICES)
    def _(i):
        pl.semaphore_signal(barrier, inc=1, device_id=peer(i, 1), device_id_type=MESH)

    rows_of = CHUNK * MSG
    sub = rem(iota((rows_of, BLOCK), 0), MSG).astype(F32)
    first = sub < 4.0

    def peers_of(c):
        return pl.ds(c * CHUNK, CHUNK)

    def flat(ref, cols):
        part = ref[:, :, cols].astype(F32)
        return part.reshape(rows_of, part.shape[2]).astype(BF)

    def stacked(rows):
        return rows.reshape(CHUNK, MSG, rows.shape[1]).astype(BF)

    def spread(ref, c):
        rows = ref[pl.ds(pl.multiple_of(c * CHUNK, CHUNK), CHUNK), :]
        return jnp.broadcast_to(rows[:, None, :], (CHUNK, MSG, BLOCK)).reshape(rows_of, BLOCK)

    def hits(c):
        slot = spread(slot_of, c)
        return slot == sub, first & (slot == sub + 8.0), (~first) & (slot == sub + 4.0)

    def as_one(mask):
        return jnp.where(mask, 1.0, 0.0).astype(BF)

    def outbound(i, sign, source, target, s_sem, r_sem):
        c = div(i, CHUNK)
        return pltpu.make_async_remote_copy(
            src_ref=source.at[i], dst_ref=target.at[i],
            send_sem=s_sem.at[c], recv_sem=r_sem.at[c],
            device_id=peer(i, sign), device_id_type=MESH,
        )

    def to_self(source, target, sem):
        return pltpu.make_async_copy(source.at[0], target.at[0], sem.at[0])

    def start_all(c, sign, source, target, s_sem, r_sem):
        @pl.when(c == 0)
        def _():
            to_self(source, target, r_sem).start()

        @pl.loop(jnp.maximum(c * CHUNK, 1), (c + 1) * CHUNK)
        def _(i):
            outbound(i, sign, source, target, s_sem, r_sem).start()

    def take(c, source, sem):
        group = source.at[peers_of(c)]
        pltpu.make_async_copy(group, group, sem.at[c]).wait()
        copy = pltpu.make_async_copy(group, part, part_sem)
        copy.start()
        copy.wait()

    def fill(c):
        whole, low, high = hits(c)
        send[peers_of(c), :, 0:D] = stacked(dot(as_one(whole), normed[...]))
        halves = dot(as_one(low), normed[:, 0 : D // 2]) + dot(as_one(high), normed[:, D // 2 :])
        send[peers_of(c), :, D:] = stacked(halves)

    fill(0)
    pl.semaphore_wait(barrier, DEVICES - 1)
    start_all(0, 1, send, recv, send_sem, recv_sem)

    @pl.loop(1, CHUNKS)
    def _(c):
        fill(c)
        start_all(c, 1, send, recv, send_sem, recv_sem)

    up_copy.wait()
    down_copy.wait()
    quarter = CHUNK * 4
    r, k = iota((quarter, rows_of), 1), iota((quarter, rows_of), 0)
    where = div(k, 4) * MSG + rem(k, 4)
    pick_low, pick_high = as_one(r == where), as_one(r == where + 4)
    r, k = iota((rows_of, quarter), 0), iota((rows_of, quarter), 1)
    where = div(k, 4) * MSG + rem(k, 4)
    put_low, put_high = as_one(r == where), as_one(r == where + 4)

    @pl.loop(0, CHUNKS)
    def _(c):
        take(c, recv, recv_sem)
        x_ref[0:rows_of] = flat(part, slice(0, D))
        halves = flat(part, slice(D, MSG_COLS))
        x_ref[rows_of:, 0 : D // 2] = dot(pick_low, halves).astype(BF)
        x_ref[rows_of:, D // 2 :] = dot(pick_high, halves).astype(BF)
        projected = dot(x_ref[...], w_up[...])
        gate = projected[:, 0:FF]
        hidden = (gate / (1.0 + jnp.exp(-gate)) * projected[:, FF:]).astype(BF)
        result = dot(hidden, w_down[...])
        back[peers_of(c), :, 0:D] = stacked(result[0:rows_of])
        rest = result[rows_of:].astype(BF)
        back[peers_of(c), :, D:] = stacked(dot(put_low, rest[:, 0 : D // 2]) + dot(put_high, rest[:, D // 2 :]))
        start_all(c, -1, back, ret, back_sem, ret_sem)

    total[...] = state[...]

    def weighted(mask, weight):
        exact = jnp.where(mask, weight, 0.0)
        high = exact.astype(BF)
        return high, (exact - high.astype(F32)).astype(BF)

    def turned(a, b):
        return lax.dot_general(a, b, (((0,), (0,)), ((), ())), preferred_element_type=F32)

    @pl.loop(0, CHUNKS)
    def _(c):
        take(c, ret, ret_sem)
        weight = spread(weight_of, c)
        whole, low, high = hits(c)
        for mask, source, target in (
            (whole, slice(0, D), slice(0, D)),
            (low, slice(D, MSG_COLS), slice(0, D // 2)),
            (high, slice(D, MSG_COLS), slice(D // 2, D)),
        ):
            coarse, fine = weighted(mask, weight)
            rows = flat(part, source)
            total[:, target] += turned(coarse, rows) + turned(fine, rows)

    mixed[...] = total[...].astype(BF)
    for c in range(CHUNKS):
        rows = pl.ds(1 if c == 0 else c * CHUNK, CHUNK - (1 if c == 0 else 0))
        pltpu.make_async_copy(send.at[rows], send.at[rows], send_sem.at[c]).wait()
        pltpu.make_async_copy(back.at[rows], back.at[rows], back_sem.at[c]).wait()


def experts(normed, state, slot_of, weight_of, w_gate_up, w_down):
    vmem = pl.BlockSpec(memory_space=pltpu.VMEM)
    hbm = pl.BlockSpec(memory_space=pl.ANY)
    messages = (DEVICES, MSG, MSG_COLS)
    sems = pltpu.SemaphoreType.DMA((CHUNKS,))
    return pl.pallas_call(
        expert_kernel,
        out_shape=(
            jax.ShapeDtypeStruct((BLOCK, D), BF),
            jax.ShapeDtypeStruct(messages, BF),
            jax.ShapeDtypeStruct(messages, BF),
        ),
        in_specs=[vmem] * 4 + [hbm] * 2,
        out_specs=(vmem, hbm, hbm),
        scratch_shapes=[
            pltpu.VMEM(messages, BF),
            pltpu.VMEM(messages, BF),
            pltpu.VMEM((D, 2 * FF), BF),
            pltpu.VMEM((FF, D), BF),
            pltpu.VMEM((CHUNK * 12, D), BF),
            pltpu.VMEM((CHUNK, MSG, MSG_COLS), BF),
            pltpu.VMEM((BLOCK, D), F32),
            pltpu.SemaphoreType.DMA((2,)),
            sems, sems, sems, sems,
            pltpu.SemaphoreType.DMA,
        ],
        compiler_params=pltpu.CompilerParams(
            collective_id=1, has_side_effects=True, vmem_limit_bytes=56 << 20
        ),
        name="experts",
    )(normed, state, slot_of, weight_of, w_gate_up, w_down)[0]


def slots(routes, gate_codes):
    slot = jnp.arange(DEVICES, dtype=jnp.int32)
    g, s, d = peer(slot, 1)
    expert = (g * 32 + s * 8 + d)[:, None]
    codes = gate_codes.astype(F32)
    weight = (codes / jnp.sum(codes, axis=-1, keepdims=True)).T
    chosen = routes.T
    hit = jnp.zeros((DEVICES, BLOCK), jnp.bool_)
    weight_of = jnp.zeros((DEVICES, BLOCK), F32)
    for j in range(TOP):
        here = chosen[j][None, :] == expert
        hit = hit | here
        weight_of = weight_of + jnp.where(here, weight[j][None, :], 0.0)
    earlier = (iota((BLOCK, BLOCK), 0) < iota((BLOCK, BLOCK), 1)).astype(BF)
    rank = dot(hit.astype(BF), earlier)
    return jnp.where(hit, rank, -1.0), weight_of


def per_device(
    queries, cached, new_entries, lengths, residual, w_out, norm_gain, w_gate_up, w_down, routes, gate_codes
):
    slot_of, weight_of = slots(routes[0], gate_codes[0])
    attn_out, state, normed = attend_and_norm(
        lengths, queries[0, 0], cached[0, 0], new_entries[0, 0], residual[0], norm_gain[None, :], w_out
    )
    mixed = experts(normed, state, slot_of, weight_of, w_gate_up[0], w_down[0])
    return attn_out[None], mixed[None]


def solution(mesh):
    rows = P(("sub", "dev"), "grp", None)
    heads = P("grp", ("sub", "dev"), None, None)
    expert = P(("grp", "sub", "dev"), None, None)
    placed = (
        heads, heads, heads, P(("sub", "dev")), rows, P("grp", None), P(), expert, expert, rows, rows,
    )
    return jax.shard_map(per_device, mesh=mesh, in_specs=placed, out_specs=(rows, rows), check_vma=False)
```

time: 473 us -> 239 us (0.51)
  the two profiles are of different devices: /device:TPU:90 before, /device:TPU:42 now
where the time goes in v1:
time: 239 us; the launch traced here: 238 us
  Pallas kernels  230 us (96%)
  local copies, waits for them, and re-layouts  3.67 us (2%)
    pallas_call x1, Pallas kernels, experts(): pl.pallas_call(expert_kernel, out_shape=(jax.ShapeDtypeStruct((BLOCK, D),...  181 us
    pallas_call x1, Pallas kernels, attend_and_norm(): pl.pallas_call(attend_kernel, out_shape=(jax.ShapeDtypeStruct(block, BF),...  49.5 us

profile of v1, /device:TPU:42, one launch (start us, length us, event | category | flops | bytes accessed | tf_op | source)
XLA Modules:
  0.0 238.5 jit_solution(11291824371368168439)
XLA Ops:
  1.3 0.7 convert_reduce_fusion
  2.0 0.7 fusion.16
  2.7 1.0 slice_bitcast_fusion.15
  3.7 0.7 fusion.6.weight_of
  4.5 0.9 convolution_select_fusion.slot_of
  5.3 49.5 %attend_and_norm.1 = (bf16[128,2048]{1,0:T(8,128)(2,1)}, f32[128,2048]{1,0:T(8,128)}, bf16[128,2048]{1,0:T(8,128)(2,1)}) custom-call(s32[1]{0:T(128)S(6)} %copy.15.length, bf16[512,1024]{1,0:T(8,128)(2,1)} %bitcast.53, bf16[4096,256]{1,0:T(8,128)(2,1)} %bitcast.52, bf16[512,256]{1,0:T(8,128)(2,1)} %bitcast.57, bf16[128,2048]{1,0:T(8,128)(2,1)} %bitcast.54, ...), custom_call_target="tpu_custom_call" | custom-call | tf_op jit(solution)/shard_map/attend_and_norm/pallas_call | solution.py:158
  54.8 0.0 copy-start
  54.8 181.0 %experts.1 = (bf16[128,2048]{1,0:T(8,128)(2,1)}, bf16[128,8,3072]{2,1,0:T(8,128)(2,1)}, bf16[128,8,3072]{2,1,0:T(8,128)(2,1)}) custom-call(bf16[128,2048]{1,0:T(8,128)(2,1)} %get-tuple-element.7.normed, f32[128,2048]{1,0:T(8,128)} %get-tuple-element.8.state, f32[128,128]{1,0:T(8,128)} %convolution_select_fusion.slot_of, f32[128,128]{1,0:T(8,128)} %fusion.6.weight_of, ...), custom_call_target="tpu_custom_call" | custom-call | tf_op jit(solution)/shard_map/experts/pallas_call | solution.py:335
  235.8 0.0 copy-done
  235.8 0.8 copy.16
  236.6 1.9 copy.17
  (2 shorter events, 0.0 us)
Async XLA Ops:
  54.8 181.0 %copy-start = (bf16[128,2048]{1,0:T(8,128)(2,1)S(1)}, bf16[128,2048]{1,0:T(8,128)(2,1)}, u32[]{:S(2)}) copy-start(bf16[128,2048]{1,0:T(8,128)(2,1)} %get-tuple-element.6) | copy-start | bytes 1572868

commit v2 on v1

v2 whole, which is shorter than its diff:
```python
import functools

import jax
import jax.numpy as jnp
from jax import lax
from jax.experimental import pallas as pl
from jax.experimental.pallas import tpu as pltpu
from jax.sharding import PartitionSpec as P

MESH = pl.DeviceIdType.MESH
TOP = 8
D = 2048
FF = 768
HD = 128
HEADS = 8
CACHE = 4096
SPAN = 512
KEYS = CACHE + SPAN
BLOCK = 128
UNIT = 512
TILE = 512
SCALE = HD**-0.5 * 1.4426950408889634
HIDDEN = -1e30
DEVICES = 128
PLANE = 32
LINE = 4
AXES = 3
STRIDE = 11
MSG = 8
PARTS = ((0, 640), (640, 640), (1280, 768))
LOW = 384
CHUNK = 32
CHUNKS = DEVICES // CHUNK
BF = jnp.bfloat16
F32 = jnp.float32


def iota(shape, dim):
    return lax.broadcasted_iota(jnp.int32, shape, dim)


def rem(a, b):
    return lax.rem(a, jnp.int32(b))


def div(a, b):
    return lax.div(a, jnp.int32(b))


def place(offset, sign):
    g, s, d = lax.axis_index("grp"), lax.axis_index("sub"), lax.axis_index("dev")
    og, os, ox, oc = offset
    x = rem(div(d, 2) + sign * ox + 4, 4)
    return rem(g + sign * og + 4, 4), rem(s + sign * os + 4, 4), x * 2 + rem(rem(d, 2) + oc, 2)


def along(axis, step):
    return tuple(step if k == axis else 0 for k in range(AXES)) + (0,)


def across(axis, p):
    a, b, c = div(p, 8), rem(div(p, 2), 4), rem(p, 2)
    return ((0, a, b, c), (a, 0, b, c), (a, b, 0, c))[axis]


def source_at(axis, member, p):
    if axis == 0:
        return member * 32 + p
    if axis == 1:
        return div(p, 8) * 32 + member * 8 + rem(p, 8)
    return div(p, 2) * 8 + member * 2 + rem(p, 2)


def member_and_place(axis, source):
    if axis == 0:
        return div(source, 32), rem(source, 32)
    if axis == 1:
        return rem(div(source, 8), 4), div(source, 32) * 8 + rem(source, 8)
    return rem(div(source, 2), 4), div(source, 8) * 2 + rem(source, 2)


def mixed_place(step):
    o = rem(step * STRIDE, PLANE)
    return rem(o, 4) * 8 + rem(div(o, 4), 4) * 2 + div(o, 16)


def dot(a, b):
    return jnp.dot(a, b, preferred_element_type=F32)


def attend_kernel(
    length, q_ref, cached, new, residual, gain, choices, w_hbm,
    out_ref, state_ref, normed_ref, slot_of, weight_of,
    keys, values, queries, scores, probs, peaks, attended, w_ref, sent, arrived, own, lines,
    w_sem, send_sem, recv_sem, line_send, line_recv,
):
    g, s, d = lax.axis_index("grp"), lax.axis_index("sub"), lax.axis_index("dev")
    w_copy = pltpu.make_async_copy(w_hbm, w_ref, w_sem)
    w_copy.start()
    barrier = pltpu.get_barrier_semaphore()
    for axis in range(AXES):
        for step in range(1, LINE):
            pl.semaphore_signal(barrier, inc=1, device_id=place(along(axis, step), 1), device_id_type=MESH)

    ones = jnp.where(iota((TILE, HD), 1) == 0, 1.0, 0.0).astype(BF)

    @pl.loop(0, CACHE // TILE)
    def _(i):
        rows = pl.ds(pl.multiple_of(i * TILE, TILE), TILE)
        keys[0:HD, rows] = cached[rows, 0:HD].T
        unseen = (iota((HD, TILE), 0) == 0) & (i * TILE + iota((HD, TILE), 1) >= length[0])
        keys[HD:, rows] = jnp.where(unseen, HIDDEN, 0.0).astype(BF)
        values[rows, 0:HD] = cached[rows, HD:]
        values[rows, HD:] = ones

    keys[0:HD, CACHE:] = new[:, 0:HD].T
    keys[HD:, CACHE:] = jnp.zeros((HD, SPAN), BF)
    values[CACHE:, 0:HD] = new[:, HD:]
    values[CACHE:, HD:] = ones
    for slot in range(2):
        queries[slot, :, HD:] = jnp.where(iota((UNIT, HD), 1) == 0, 1.0, 0.0).astype(BF)

    def score(step, slot):
        block = rem(g + 1 + step, 4)
        rows = pl.ds(pl.multiple_of(block * BLOCK, BLOCK), BLOCK)
        for k in range(4):
            head = slot * 4 + k
            queries[slot, k * BLOCK : (k + 1) * BLOCK, 0:HD] = q_ref[rows, head * HD : (head + 1) * HD]
        q = queries[slot]
        peak = None
        for j in range(KEYS // TILE):
            tile = dot(q, keys[:, j * TILE : (j + 1) * TILE])
            if j * TILE >= CACHE:
                row = block * BLOCK + rem(iota((UNIT, TILE), 0), BLOCK)
                tile = jnp.where(iota((UNIT, TILE), 1) + (j * TILE - CACHE) <= row, tile, HIDDEN)
            scores[slot, :, j * TILE : (j + 1) * TILE] = tile
            for k in range(TILE // HD):
                part = tile[:, k * HD : (k + 1) * HD]
                peak = part if peak is None else jnp.maximum(peak, part)
        peaks[slot] = jnp.broadcast_to(jnp.max(peak, axis=1, keepdims=True), (UNIT, HD))

    def finish(slot):
        peak = peaks[slot]
        for k in range(KEYS // HD):
            cols = slice(k * HD, (k + 1) * HD)
            probs[:, cols] = jnp.exp2((scores[slot, :, cols] - peak) * SCALE).astype(BF)
        total = dot(probs[...], values[...])
        result = (total[:, 0:HD] / total[:, HD : HD + 1]).astype(BF)
        for k in range(4):
            head = slot * 4 + k
            attended[:, head * HD : (head + 1) * HD] = result[k * BLOCK : (k + 1) * BLOCK]

    def hand_over(step):
        block = rem(g + 1 + step, 4)
        return pltpu.make_async_remote_copy(
            src_ref=sent.at[step], dst_ref=arrived.at[step],
            send_sem=send_sem.at[step], recv_sem=recv_sem.at[step],
            device_id=(block, s, d), device_id_type=MESH,
        )

    def tell(axis, member):
        at = axis * (LINE - 1) + member - 1
        return pltpu.make_async_remote_copy(
            src_ref=choices, dst_ref=lines.at[at],
            send_sem=line_send.at[at], recv_sem=line_recv.at[at],
            device_id=place(along(axis, member), 1), device_id_type=MESH,
        )

    pairs = [(axis, member) for axis in range(AXES) for member in range(1, LINE)]
    score(0, 0)
    w_copy.wait()
    pl.semaphore_wait(barrier, len(pairs))
    for axis, member in pairs:
        tell(axis, member).start()

    @pl.loop(0, 4)
    def _(step):
        score(step, 1)
        finish(0)
        score(jnp.minimum(step + 1, 3), 0)
        finish(1)
        own[...] = dot(attended[...], w_ref[...])

        @pl.when(step < 3)
        def _():
            sent[step] = own[...].astype(BF)
            hand_over(step).start()

    for axis, member in pairs:
        tell(axis, member).wait()
    earlier = jnp.where(iota((BLOCK, BLOCK), 0) < iota((BLOCK, BLOCK), 1), 1.0, 0.0).astype(BF)
    p = iota((PLANE, BLOCK), 0)
    a, b, core = p >> 3, (p >> 1) & 3, (p + d) & 1
    x = div(d, 2)
    for axis in range(AXES):
        z, y, w = ((0, a, b), (a, 0, b), (a, b, 0))[axis]
        expert = (((g + z) & 3) * 32 + ((s + y) & 3) * 8 + ((x + w) & 3) * 2 + core).astype(F32)
        for member in range(LINE):
            chosen = choices[...] if member == 0 else lines[axis * (LINE - 1) + member - 1]
            hit = jnp.zeros((PLANE, BLOCK), F32)
            weight = jnp.zeros((PLANE, BLOCK), F32)
            for j in range(TOP):
                here = chosen[j : j + 1] == expert
                hit = jnp.where(here, 1.0, hit)
                weight = jnp.where(here, chosen[TOP + j : TOP + j + 1], weight)
            rows = slice((axis * LINE + member) * PLANE, (axis * LINE + member + 1) * PLANE)
            slot_of[rows] = jnp.where(hit > 0.0, dot(hit.astype(BF), earlier), -1.0)
            weight_of[rows] = weight
    for step in range(3):
        hand_over(step).wait()
    attn_sum = own[...] + (arrived[0].astype(F32) + (arrived[1].astype(F32) + arrived[2].astype(F32)))
    out_ref[...] = attn_sum.astype(BF)
    state = residual[...].astype(F32) + attn_sum
    state_ref[...] = state
    inverse = lax.rsqrt(jnp.mean(state * state, axis=1, keepdims=True) + 1e-6)
    normed_ref[...] = (state * inverse * gain[...]).astype(BF)


def attend_and_norm(length, queries, cached, new, residual, gain, choices, w_out):
    vmem = pl.BlockSpec(memory_space=pltpu.VMEM)
    block = (BLOCK, D)
    return pl.pallas_call(
        attend_kernel,
        out_shape=(
            jax.ShapeDtypeStruct(block, BF),
            jax.ShapeDtypeStruct(block, F32),
            jax.ShapeDtypeStruct(block, BF),
            jax.ShapeDtypeStruct((AXES * LINE * PLANE, BLOCK), F32),
            jax.ShapeDtypeStruct((AXES * LINE * PLANE, BLOCK), F32),
        ),
        in_specs=[pl.BlockSpec(memory_space=pltpu.SMEM)] + [vmem] * 6 + [pl.BlockSpec(memory_space=pl.ANY)],
        out_specs=(vmem,) * 5,
        scratch_shapes=[
            pltpu.VMEM((2 * HD, KEYS), BF),
            pltpu.VMEM((KEYS, 2 * HD), BF),
            pltpu.VMEM((2, UNIT, 2 * HD), BF),
            pltpu.VMEM((2, UNIT, KEYS), F32),
            pltpu.VMEM((UNIT, KEYS), BF),
            pltpu.VMEM((2, UNIT, HD), F32),
            pltpu.VMEM((BLOCK, HEADS * HD), BF),
            pltpu.VMEM((HEADS * HD, D), BF),
            pltpu.VMEM((3, *block), BF),
            pltpu.VMEM((3, *block), BF),
            pltpu.VMEM(block, F32),
            pltpu.VMEM((AXES * (LINE - 1), 2 * TOP, BLOCK), F32),
            pltpu.SemaphoreType.DMA,
            pltpu.SemaphoreType.DMA((3,)),
            pltpu.SemaphoreType.DMA((3,)),
            pltpu.SemaphoreType.DMA((AXES * (LINE - 1),)),
            pltpu.SemaphoreType.DMA((AXES * (LINE - 1),)),
        ],
        compiler_params=pltpu.CompilerParams(
            collective_id=0, has_side_effects=True, vmem_limit_bytes=56 << 20
        ),
        name="attend_and_norm",
    )(length, queries, cached, new, residual, gain, choices, w_out)


def expert_kernel(
    normed, state, slot_of, weight_of, up_hbm, down_hbm,
    mixed, recv0, recv1, recv2, ret0, ret1, ret2,
    send0, send1, send2, back0, back1, back2, line0, line1, line2, part0, part1, part2,
    out0, out1, out2, in0, in1, in2, w_up, w_down, x_ref, total,
    w_sem, line_send, line_recv, send_sem, recv_sem, back_sem, ret_sem, part_sem, out_sem, in_sem,
):
    recv, ret, send, back = (recv0, recv1, recv2), (ret0, ret1, ret2), (send0, send1, send2), (back0, back1, back2)
    line, part, leaving, coming = (line0, line1, line2), (part0, part1, part2), (out0, out1, out2), (in0, in1, in2)
    up_copy = pltpu.make_async_copy(up_hbm, w_up, w_sem.at[0])
    down_copy = pltpu.make_async_copy(down_hbm, w_down, w_sem.at[1])
    up_copy.start()
    down_copy.start()
    barrier = pltpu.get_barrier_semaphore()

    @pl.loop(1, DEVICES)
    def _(i):
        offset = (div(i, 32), rem(div(i, 8), 4), rem(div(i, 2), 4), rem(i, 2))
        pl.semaphore_signal(barrier, inc=1, device_id=place(offset, 1), device_id_type=MESH)

    rows_of = CHUNK * MSG
    sub = rem(iota((rows_of, BLOCK), 0), MSG).astype(F32)
    first = sub < 4.0
    for axis, (start, cols) in enumerate(PARTS):
        line[axis][0] = normed[:, start : start + cols]

    def flat(values):
        return values.astype(F32).reshape(rows_of, values.shape[2]).astype(BF)

    def stacked(rows):
        return rows.reshape(CHUNK, MSG, rows.shape[1]).astype(BF)

    def widened(rows):
        if rows.shape[1] == LOW:
            return rows
        return jnp.concatenate([rows, jnp.zeros((rows.shape[0], LOW - rows.shape[1]), F32)], axis=1)

    def spread(ref, axis, member):
        rows = ref[pl.ds(pl.multiple_of((axis * LINE + member) * PLANE, PLANE), PLANE), :]
        return jnp.broadcast_to(rows[:, None, :], (PLANE, MSG, BLOCK)).reshape(rows_of, BLOCK)

    def hits(axis, member):
        slot = spread(slot_of, axis, member)
        return slot == sub, first & (slot == sub + 8.0), (~first) & (slot == sub + 4.0)

    def as_one(mask):
        return jnp.where(mask, 1.0, 0.0).astype(BF)

    def share(axis, member):
        at = axis * (LINE - 1) + member - 1
        return pltpu.make_async_remote_copy(
            src_ref=line[axis].at[0], dst_ref=line[axis].at[member],
            send_sem=line_send.at[at], recv_sem=line_recv.at[at],
            device_id=place(along(axis, member), 1), device_id_type=MESH,
        )

    def outward(axis, member, p):
        return pltpu.make_async_remote_copy(
            src_ref=send[axis].at[member, p], dst_ref=recv[axis].at[source_at(axis, member, p)],
            send_sem=send_sem.at[axis], recv_sem=recv_sem.at[axis],
            device_id=place(across(axis, p), 1), device_id_type=MESH,
        )

    def homeward(axis, source):
        member, p = member_and_place(axis, source)
        return p, pltpu.make_async_remote_copy(
            src_ref=back[axis].at[source], dst_ref=ret[axis].at[member, p],
            send_sem=back_sem.at[axis], recv_sem=ret_sem.at[axis * LINE + member],
            device_id=place(across(axis, p), -1), device_id_type=MESH,
        ), pltpu.make_async_copy(
            back[axis].at[source], ret[axis].at[member, p], ret_sem.at[axis * LINE + member]
        )

    def go_home(axis, source):
        p, away, here = homeward(axis, source)

        @pl.when(p > 0)
        def _():
            away.start()

        @pl.when(p == 0)
        def _():
            here.start()

    def settle(axis, member):
        at = axis * (LINE - 1) + member - 1
        return pltpu.make_async_remote_copy(
            src_ref=leaving[axis].at[member - 1], dst_ref=coming[axis].at[member - 1],
            send_sem=out_sem.at[at], recv_sem=in_sem.at[at],
            device_id=place(along(axis, member), -1), device_id_type=MESH,
        )

    def take(sources):
        copies = [pltpu.make_async_copy(source, part[axis], part_sem.at[axis]) for axis, source in sources]
        for copy in copies:
            copy.start()
        for copy in copies:
            copy.wait()

    pl.semaphore_wait(barrier, DEVICES - 1)
    for member in range(1, LINE):
        for axis in range(AXES):
            share(axis, member).start()

    @pl.loop(0, LINE)
    def _(member):
        @pl.when(member > 0)
        def _():
            for axis in range(AXES):
                share(axis, member).wait_recv()

        for axis, (start, cols) in enumerate(PARTS):
            whole, low, high = hits(axis, member)
            rows = line[axis][member]
            send[axis][member, :, :, 0:cols] = stacked(dot(as_one(whole), rows))
            rest = dot(as_one(low), rows[:, 0:LOW]) + widened(dot(as_one(high), rows[:, LOW:]))
            send[axis][member, :, :, cols:] = stacked(rest)
            pltpu.make_async_copy(
                send[axis].at[member, 0], recv[axis].at[source_at(axis, member, 0)], recv_sem.at[axis]
            ).start()

        @pl.loop(1, PLANE)
        def _(step):
            p = mixed_place(step)
            for axis in range(AXES):
                outward(axis, member, p).start()

    up_copy.wait()
    down_copy.wait()
    total[...] = state[...]
    quarter = CHUNK * 4
    r, k = iota((quarter, rows_of), 1), iota((quarter, rows_of), 0)
    where = (k >> 2) * MSG + (k & 3)
    pick_low, pick_high = as_one(r == where), as_one(r == where + 4)
    r, k = iota((rows_of, quarter), 0), iota((rows_of, quarter), 1)
    where = (k >> 2) * MSG + (k & 3)
    put_low, put_high = as_one(r == where), as_one(r == where + 4)
    for axis in range(AXES):
        pltpu.make_async_copy(recv[axis], recv[axis], recv_sem.at[axis]).wait()

    @pl.loop(0, CHUNKS)
    def _(c):
        take([(axis, recv[axis].at[pl.ds(c * CHUNK, CHUNK)]) for axis in range(AXES)])
        for axis, (start, cols) in enumerate(PARTS):
            x_ref[0:rows_of, start : start + cols] = flat(part[axis][:, :, 0:cols])
            rest = flat(part[axis][:, :, cols:])
            x_ref[rows_of:, start : start + LOW] = dot(pick_low, rest).astype(BF)
            x_ref[rows_of:, start + LOW : start + cols] = dot(pick_high, rest[:, 0 : cols - LOW]).astype(BF)
        projected = dot(x_ref[...], w_up[...])
        gate = projected[:, 0:FF]
        hidden = (gate / (1.0 + jnp.exp(-gate)) * projected[:, FF:]).astype(BF)
        result = dot(hidden, w_down[...])
        cut = result[rows_of:].astype(BF)
        for axis, (start, cols) in enumerate(PARTS):
            back[axis][pl.ds(c * CHUNK, CHUNK), :, 0:cols] = stacked(result[0:rows_of, start : start + cols])
            rest = dot(put_low, cut[:, start : start + LOW])
            rest = rest + widened(dot(put_high, cut[:, start + LOW : start + cols]))
            back[axis][pl.ds(c * CHUNK, CHUNK), :, cols:] = stacked(rest)

        @pl.loop(0, PLANE)
        def _(step):
            source = c * CHUNK + mixed_place(step)
            for axis in range(AXES):
                member = member_and_place(axis, source)[0]

                @pl.when(member > 0)
                def _():
                    go_home(axis, source)

    @pl.loop(0, PLANE)
    def _(step):
        p = mixed_place(step)
        for axis in range(AXES):
            go_home(axis, source_at(axis, 0, p))

    def combine(axis, member):
        cols = PARTS[axis][1]
        group = ret[axis].at[member]
        pltpu.make_async_copy(group, group, ret_sem.at[axis * LINE + member]).wait()
        take([(axis, group)])
        weight = spread(weight_of, axis, member)

        def summed(mask, rows):
            exact = jnp.where(mask, weight, 0.0)
            coarse = exact.astype(BF)
            fine = (exact - coarse.astype(F32)).astype(BF)
            both = jnp.concatenate([coarse, fine], axis=1)
            out = lax.dot_general(both, rows, (((0,), (0,)), ((), ())), preferred_element_type=F32)
            return out[0:BLOCK] + out[BLOCK:]

        whole, low, high = hits(axis, member)
        rest = flat(part[axis][:, :, cols:])
        halves = jnp.concatenate([summed(low, rest), summed(high, rest[:, 0 : cols - LOW])], axis=1)
        return summed(whole, flat(part[axis][:, :, 0:cols])) + halves

    @pl.loop(1, LINE)
    def _(member):
        for axis in range(AXES):
            leaving[axis][member - 1] = combine(axis, member).astype(BF)
            settle(axis, member).start()

    for axis, (start, cols) in enumerate(PARTS):
        total[:, start : start + cols] += combine(axis, 0)

    for axis, (start, cols) in enumerate(PARTS):
        for member in range(1, LINE):
            settle(axis, member).wait()
            total[:, start : start + cols] += coming[axis][member - 1].astype(F32)
    mixed[...] = total[...].astype(BF)
    for axis in range(AXES):
        for member in range(1, LINE):
            share(axis, member).wait_send()
        rows = send[axis].at[:, pl.ds(1, PLANE - 1)]
        pltpu.make_async_copy(rows, rows, send_sem.at[axis]).wait()
        rows = back[axis].at[pl.ds(LINE, DEVICES - LINE)]
        pltpu.make_async_copy(rows, rows, back_sem.at[axis]).wait()


def experts(normed, state, slot_of, weight_of, w_gate_up, w_down):
    vmem = pl.BlockSpec(memory_space=pltpu.VMEM)
    hbm = pl.BlockSpec(memory_space=pl.ANY)
    wide = [(MSG, cols + LOW) for _, cols in PARTS]
    by_source = [(DEVICES, *w) for w in wide]
    by_place = [(LINE, PLANE, *w) for w in wide]
    sems = pltpu.SemaphoreType.DMA((AXES,))
    pair_sems = pltpu.SemaphoreType.DMA((AXES * (LINE - 1),))
    return pl.pallas_call(
        expert_kernel,
        out_shape=tuple(jax.ShapeDtypeStruct(shape, BF) for shape in [(BLOCK, D), *by_source, *by_place]),
        in_specs=[vmem] * 4 + [hbm] * 2,
        out_specs=(vmem,) + (hbm,) * 6,
        scratch_shapes=[
            *(pltpu.VMEM(shape, BF) for shape in by_place),
            *(pltpu.VMEM(shape, BF) for shape in by_source),
            *(pltpu.VMEM((LINE, BLOCK, cols), BF) for _, cols in PARTS),
            *(pltpu.VMEM((CHUNK, *w), BF) for w in wide),
            *(pltpu.VMEM((LINE - 1, BLOCK, cols), BF) for _, cols in PARTS),
            *(pltpu.VMEM((LINE - 1, BLOCK, cols), BF) for _, cols in PARTS),
            pltpu.VMEM((D, 2 * FF), BF),
            pltpu.VMEM((FF, D), BF),
            pltpu.VMEM((CHUNK * 12, D), BF),
            pltpu.VMEM((BLOCK, D), F32),
            pltpu.SemaphoreType.DMA((2,)),
            pair_sems, pair_sems, sems, sems, sems,
            pltpu.SemaphoreType.DMA((AXES * LINE,)),
            sems, pair_sems, pair_sems,
        ],
        compiler_params=pltpu.CompilerParams(
            collective_id=1, has_side_effects=True, vmem_limit_bytes=56 << 20
        ),
        name="experts",
    )(normed, state, slot_of, weight_of, w_gate_up, w_down)[0]


def per_device(
    queries, cached, new_entries, lengths, residual, w_out, norm_gain, w_gate_up, w_down, routes, gate_codes
):
    codes = gate_codes[0].astype(F32)
    weight = codes / jnp.sum(codes, axis=-1, keepdims=True)
    choices = jnp.concatenate([routes[0].astype(F32), weight], axis=1).T
    attn_out, state, normed, slot_of, weight_of = attend_and_norm(
        lengths, queries[0, 0], cached[0, 0], new_entries[0, 0], residual[0], norm_gain[None, :], choices, w_out
    )
    mixed = experts(normed, state, slot_of, weight_of, w_gate_up[0], w_down[0])
    return attn_out[None], mixed[None]


def solution(mesh):
    rows = P(("sub", "dev"), "grp", None)
    heads = P("grp", ("sub", "dev"), None, None)
    expert = P(("grp", "sub", "dev"), None, None)
    placed = (
        heads, heads, heads, P(("sub", "dev")), rows, P("grp", None), P(), expert, expert, rows, rows,
    )
    return jax.shard_map(per_device, mesh=mesh, in_specs=placed, out_specs=(rows, rows), check_vma=False)
```

time: 239 us -> 218 us (0.912)
  the two profiles are of different devices: /device:TPU:42 before, /device:TPU:1 now
where the time goes in v2:
time: 218 us; the launch traced here: 217 us
  Pallas kernels  210 us (96%)
  other arithmetic  2.69 us (1%)
  local copies, waits for them, and re-layouts  2.68 us (1%)
    pallas_call x1, Pallas kernels, experts(): pl.pallas_call(expert_kernel, out_shape=tuple((jax.ShapeDtypeStruct(shape...  161 us
    pallas_call x1, Pallas kernels, attend_and_norm(): pl.pallas_call(attend_kernel, out_shape=(jax.ShapeDtypeStruct(block, BF),...  49 us

profile of v2, /device:TPU:1, one launch (start us, length us, event | category | flops | bytes accessed | tf_op | source)
XLA Modules:
  0.0 217.1 jit_solution(7205040972347230390)
XLA Ops:
  1.3 0.7 convert_reduce_fusion
  2.0 0.7 bitcast_divide_fusion
  2.7 0.7 convert_bitcast_fusion
  3.4 0.6 maximum_bitcast_fusion.choices
  4.0 49.0 %attend_and_norm.1 = (bf16[128,2048]{1,0:T(8,128)(2,1)}, f32[128,2048]{1,0:T(8,128)}, bf16[128,2048]{1,0:T(8,128)(2,1)}, f32[384,128]{1,0:T(8,128)}, f32[384,128]{1,0:T(8,128)}) custom-call(s32[1]{0:T(128)S(6)} %copy.15.length, bf16[512,1024]{1,0:T(8,128)(2,1)} %bitcast.18, bf16[4096,256]{1,0:T(8,128)(2,1)} %bitcast.17, bf16[512,256]{1,0:T(8,128)(2,1)} %bitcast.22, ...), custom_call_target="tpu_custom_call" | custom-call | tf_op jit(solution)/shard_map/attend_and_norm/pallas_call | solution.py:222
  52.9 0.0 copy-start
  53.0 161.4 %experts.1 = (bf16[128,2048]{1,0:T(8,128)(2,1)}, bf16[128,8,1024]{2,1,0:T(8,128)(2,1)}, bf16[128,8,1024]{2,1,0:T(8,128)(2,1)}, bf16[128,8,1152]{2,1,0:T(8,128)(2...) custom-call(bf16[128,2048]{1,0:T(8,128)(2,1)} %get-tuple-element.9.normed,, ...), custom_call_target="tpu_custom_call" | custom-call | tf_op jit(solution)/shard_map/experts/pallas_call | solution.py:485
  214.4 0.0 copy-done
  214.4 0.8 copy.16
  215.2 1.9 copy.17
Async XLA Ops:
  52.9 161.4 %copy-start = (bf16[128,2048]{1,0:T(8,128)(2,1)S(1)}, bf16[128,2048]{1,0:T(8,128)(2,1)}, u32[]{:S(2)}) copy-start(bf16[128,2048]{1,0:T(8,128)(2,1)} %get-tuple-element.8) | copy-start | bytes 1572868

commit v3 on v2

--- a/solution.py
+++ b/solution.py
@@ -40,11 +40,11 @@
 
 
 def rem(a, b):
-    return lax.rem(a, jnp.int32(b))
+    return lax.rem(jnp.int32(a), jnp.int32(b))
 
 
 def div(a, b):
-    return lax.div(a, jnp.int32(b))
+    return lax.div(jnp.int32(a), jnp.int32(b))
 
 
 def place(offset, sign):
@@ -313,11 +313,13 @@
         )
 
     def outward(axis, member, p):
+        source = source_at(axis, member, p)
+        arrival = recv_sem.at[axis * CHUNKS + div(source, CHUNK)]
         return pltpu.make_async_remote_copy(
-            src_ref=send[axis].at[member, p], dst_ref=recv[axis].at[source_at(axis, member, p)],
-            send_sem=send_sem.at[axis], recv_sem=recv_sem.at[axis],
+            src_ref=send[axis].at[member, p], dst_ref=recv[axis].at[source],
+            send_sem=send_sem.at[axis], recv_sem=arrival,
             device_id=place(across(axis, p), 1), device_id_type=MESH,
-        )
+        ), pltpu.make_async_copy(send[axis].at[member, p], recv[axis].at[source], arrival)
 
     def homeward(axis, source):
         member, p = member_and_place(axis, source)
@@ -360,28 +362,63 @@
         for axis in range(AXES):
             share(axis, member).start()
 
-    @pl.loop(0, LINE)
+    def fill(axis, member):
+        cols = PARTS[axis][1]
+        whole, low, high = hits(axis, member)
+        rows = line[axis][member]
+        send[axis][member, :, :, 0:cols] = stacked(dot(as_one(whole), rows))
+        rest = dot(as_one(low), rows[:, 0:LOW]) + widened(dot(as_one(high), rows[:, LOW:]))
+        send[axis][member, :, :, cols:] = stacked(rest)
+
+    def go_out(axis, member, p):
+        away, here = outward(axis, member, p)
+
+        @pl.when(p > 0)
+        def _():
+            away.start()
+
+        @pl.when(p == 0)
+        def _():
+            here.start()
+
+    def go_out_for(c, step):
+        for axis in (1, 2):
+            go_out(axis, rem(step, LINE), c * 8 + rem(div(step, LINE) * 3, 8))
+
+    fill(0, 0)
+
+    @pl.loop(0, PLANE)
+    def _(step):
+        go_out(0, 0, mixed_place(step))
+
+    fill(1, 0)
+    fill(2, 0)
+
+    @pl.loop(1, LINE)
     def _(member):
-        @pl.when(member > 0)
-        def _():
-            for axis in range(AXES):
-                share(axis, member).wait_recv()
-
-        for axis, (start, cols) in enumerate(PARTS):
-            whole, low, high = hits(axis, member)
-            rows = line[axis][member]
-            send[axis][member, :, :, 0:cols] = stacked(dot(as_one(whole), rows))
-            rest = dot(as_one(low), rows[:, 0:LOW]) + widened(dot(as_one(high), rows[:, LOW:]))
-            send[axis][member, :, :, cols:] = stacked(rest)
-            pltpu.make_async_copy(
-                send[axis].at[member, 0], recv[axis].at[source_at(axis, member, 0)], recv_sem.at[axis]
-            ).start()
-
-        @pl.loop(1, PLANE)
-        def _(step):
-            p = mixed_place(step)
-            for axis in range(AXES):
-                outward(axis, member, p).start()
+        for axis in range(AXES):
+            share(axis, member).wait_recv()
+        for axis in (1, 2):
+            fill(axis, member)
+
+    @pl.loop(0, PLANE)
+    def _(step):
+        go_out_for(0, step)
+
+    @pl.loop(1, LINE)
+    def _(member):
+        fill(0, member)
+
+    @pl.loop(0, PLANE)
+    def _(step):
+        for c in (1, 3):
+            go_out(0, c, mixed_place(step))
+            go_out_for(c, step)
+
+    @pl.loop(0, PLANE)
+    def _(step):
+        go_out(0, 2, mixed_place(step))
+        go_out_for(2, step)
 
     up_copy.wait()
     down_copy.wait()
@@ -393,11 +430,13 @@
     r, k = iota((rows_of, quarter), 0), iota((rows_of, quarter), 1)
     where = (k >> 2) * MSG + (k & 3)
     put_low, put_high = as_one(r == where), as_one(r == where + 4)
-    for axis in range(AXES):
-        pltpu.make_async_copy(recv[axis], recv[axis], recv_sem.at[axis]).wait()
 
     @pl.loop(0, CHUNKS)
-    def _(c):
+    def _(turn):
+        c = turn + div(turn, 2) * (1 - 2 * rem(turn, 2))
+        for axis in range(AXES):
+            group = recv[axis].at[pl.ds(c * CHUNK, CHUNK)]
+            pltpu.make_async_copy(group, group, recv_sem.at[axis * CHUNKS + c]).wait()
         take([(axis, recv[axis].at[pl.ds(c * CHUNK, CHUNK)]) for axis in range(AXES)])
         for axis, (start, cols) in enumerate(PARTS):
             x_ref[0:rows_of, start : start + cols] = flat(part[axis][:, :, 0:cols])
@@ -499,7 +538,9 @@
             pltpu.VMEM((CHUNK * 12, D), BF),
             pltpu.VMEM((BLOCK, D), F32),
             pltpu.SemaphoreType.DMA((2,)),
-            pair_sems, pair_sems, sems, sems, sems,
+            pair_sems, pair_sems, sems,
+            pltpu.SemaphoreType.DMA((AXES * CHUNKS,)),
+            sems,
             pltpu.SemaphoreType.DMA((AXES * LINE,)),
             sems, pair_sems, pair_sems,
         ],

time: 218 us -> 203 us (0.931)
  Pallas kernels: 210 us -> 196 us
    pallas_call x1, Pallas kernels: 161 us -> 147 us  [experts(): pl.pallas_call(expert_kernel, out_shape=tuple((jax.ShapeDtypeStruct(shape...]
where the time goes in v3:
time: 203 us; the launch traced here: 202 us
  Pallas kernels  196 us (97%)
  other arithmetic  2.69 us (1%)
  local copies, waits for them, and re-layouts  2.68 us (1%)
    pallas_call x1, Pallas kernels, experts(): pl.pallas_call(expert_kernel, out_shape=tuple((jax.ShapeDtypeStruct(shape...  147 us
    pallas_call x1, Pallas kernels, attend_and_norm(): pl.pallas_call(attend_kernel, out_shape=(jax.ShapeDtypeStruct(block, BF),...  49 us

profile of v3, /device:TPU:1, one launch (start us, length us, event | category | flops | bytes accessed | tf_op | source)
XLA Modules:
  0.0 202.4 jit_solution(15308488651901706940)
XLA Ops:
  1.3 0.7 convert_reduce_fusion
  2.0 0.7 bitcast_divide_fusion
  2.7 0.7 convert_bitcast_fusion
  3.4 0.6 maximum_bitcast_fusion.choices
  4.0 49.0 %attend_and_norm.1 = (bf16[128,2048]{1,0:T(8,128)(2,1)}, f32[128,2048]{1,0:T(8,128)}, bf16[128,2048]{1,0:T(8,128)(2,1)}, f32[384,128]{1,0:T(8,128)}, f32[384,128]{1,0:T(8,128)}) custom-call(s32[1]{0:T(128)S(6)} %copy.15.length, bf16[512,1024]{1,0:T(8,128)(2,1)} %bitcast.18, bf16[4096,256]{1,0:T(8,128)(2,1)} %bitcast.17, bf16[512,256]{1,0:T(8,128)(2,1)} %bitcast.22, ...), custom_call_target="tpu_custom_call" | custom-call | tf_op jit(solution)/shard_map/attend_and_norm/pallas_call | solution.py:222
  52.9 0.0 copy-start
  53.0 146.7 %experts.1 = (bf16[128,2048]{1,0:T(8,128)(2,1)}, bf16[128,8,1024]{2,1,0:T(8,128)(2,1)}, bf16[128,8,1024]{2,1,0:T(8,128)(2,1)}, bf16[128,8,1152]{2,1,0:T(8,128)(2...) custom-call(bf16[128,2048]{1,0:T(8,128)(2,1)} %get-tuple-element.9.normed,, ...), custom_call_target="tpu_custom_call" | custom-call | tf_op jit(solution)/shard_map/experts/pallas_call | solution.py:524
  199.7 0.0 copy-done
  199.7 0.8 copy.16
  200.5 1.9 copy.17
Async XLA Ops:
  52.9 146.7 %copy-start = (bf16[128,2048]{1,0:T(8,128)(2,1)S(1)}, bf16[128,2048]{1,0:T(8,128)(2,1)}, u32[]{:S(2)}) copy-start(bf16[128,2048]{1,0:T(8,128)(2,1)} %get-tuple-element.8) | copy-start | bytes 1572868

commit v4 on v3

--- a/solution.py
+++ b/solution.py
@@ -88,6 +88,10 @@
     return jnp.dot(a, b, preferred_element_type=F32)
 
 
+def ahead(step):
+    return 1 + step + (1 - div(step, 2)) * (1 - 2 * rem(step, 2))
+
+
 def attend_kernel(
     length, q_ref, cached, new, residual, gain, choices, w_hbm,
     out_ref, state_ref, normed_ref, slot_of, weight_of,
@@ -121,7 +125,7 @@
         queries[slot, :, HD:] = jnp.where(iota((UNIT, HD), 1) == 0, 1.0, 0.0).astype(BF)
 
     def score(step, slot):
-        block = rem(g + 1 + step, 4)
+        block = rem(g + ahead(step), 4)
         rows = pl.ds(pl.multiple_of(block * BLOCK, BLOCK), BLOCK)
         for k in range(4):
             head = slot * 4 + k
@@ -151,7 +155,7 @@
             attended[:, head * HD : (head + 1) * HD] = result[k * BLOCK : (k + 1) * BLOCK]
 
     def hand_over(step):
-        block = rem(g + 1 + step, 4)
+        block = rem(g + ahead(step), 4)
         return pltpu.make_async_remote_copy(
             src_ref=sent.at[step], dst_ref=arrived.at[step],
             send_sem=send_sem.at[step], recv_sem=recv_sem.at[step],

time: 203 us -> 199 us (0.980)
  Pallas kernels: 196 us -> 192 us
    pallas_call x1, Pallas kernels: 49 us -> 46.2 us  [attend_and_norm(): pl.pallas_call(attend_kernel, out_shape=(jax.ShapeDtypeStruct(block, BF),...]
where the time goes in v4:
time: 199 us; the launch traced here: 198 us
  Pallas kernels  192 us (96%)
  other arithmetic  2.69 us (1%)
  local copies, waits for them, and re-layouts  2.68 us (1%)
    pallas_call x1, Pallas kernels, experts(): pl.pallas_call(expert_kernel, out_shape=tuple((jax.ShapeDtypeStruct(shape...  145 us
    pallas_call x1, Pallas kernels, attend_and_norm(): pl.pallas_call(attend_kernel, out_shape=(jax.ShapeDtypeStruct(block, BF),...  46.2 us

profile of v4, /device:TPU:1, one launch (start us, length us, event | category | flops | bytes accessed | tf_op | source)
XLA Modules:
  0.0 198.4 jit_solution(15058336997354232479)
XLA Ops:
  1.3 0.7 convert_reduce_fusion
  2.0 0.7 bitcast_divide_fusion
  2.7 0.7 convert_bitcast_fusion
  3.4 0.6 maximum_bitcast_fusion.choices
  4.0 46.2 %attend_and_norm.1 = (bf16[128,2048]{1,0:T(8,128)(2,1)}, f32[128,2048]{1,0:T(8,128)}, bf16[128,2048]{1,0:T(8,128)(2,1)}, f32[384,128]{1,0:T(8,128)}, f32[384,128]{1,0:T(8,128)}) custom-call(s32[1]{0:T(128)S(6)} %copy.15.length, bf16[512,1024]{1,0:T(8,128)(2,1)} %bitcast.18, bf16[4096,256]{1,0:T(8,128)(2,1)} %bitcast.17, bf16[512,256]{1,0:T(8,128)(2,1)} %bitcast.22, ...), custom_call_target="tpu_custom_call" | custom-call | tf_op jit(solution)/shard_map/attend_and_norm/pallas_call | solution.py:226
  50.2 0.0 copy-start
  50.2 145.5 %experts.1 = (bf16[128,2048]{1,0:T(8,128)(2,1)}, bf16[128,8,1024]{2,1,0:T(8,128)(2,1)}, bf16[128,8,1024]{2,1,0:T(8,128)(2,1)}, bf16[128,8,1152]{2,1,0:T(8,128)(2...) custom-call(bf16[128,2048]{1,0:T(8,128)(2,1)} %get-tuple-element.9.normed,, ...), custom_call_target="tpu_custom_call" | custom-call | tf_op jit(solution)/shard_map/experts/pallas_call | solution.py:528
  195.7 0.0 copy-done
  195.7 0.8 copy.16
  196.5 1.9 copy.17
Async XLA Ops:
  50.2 145.5 %copy-start = (bf16[128,2048]{1,0:T(8,128)(2,1)S(1)}, bf16[128,2048]{1,0:T(8,128)(2,1)}, u32[]{:S(2)}) copy-start(bf16[128,2048]{1,0:T(8,128)(2,1)} %get-tuple-element.8) | copy-start | bytes 1572868
